TPU v7x, 512 devices: a whole 4x4x16 slice. The times are simulated.
512 devices in a mesh: dp: 64 (over y, z_hi, x, core), fsdp: 8 (over z_lo).
Axes of the slice: x: 4, y: 4, z: 16 (z_hi: 2, z_lo: 8; z = z_hi * 8 + z_lo), core: 2. Of those that a mesh axis runs over, the one named last changes fastest.
Arguments:
- inputs: bfloat16 [65536, 4096], P(('dp', 'fsdp')), may hold values from -6 to 6
- out_grad: bfloat16 [65536, 2048], P(('dp', 'fsdp')), may hold values from -24 to 24
- weight: bfloat16 [4096, 2048], P('fsdp'), may hold values from -0.125 to 0.125
- proj_basis: bfloat16 [4096, 256], P('fsdp'), may hold values from -0.09375 to 0.09375
- first_moment: float32 [64, 8192], P('dp'), may hold values from -6 to 6
- second_moment: float32 [64, 8192], P('dp'), may hold values from 0.25 to 4
Outputs:
- input_grad: bfloat16 [65536, 4096], P(('dp', 'fsdp'))
- new_first: float32 [64, 8192], P('dp')
- new_second: float32 [64, 8192], P('dp')
- update: float32 [4096, 2048], P('fsdp', 'dp')
All inputs are finite; a program needn't handle non-finite values.
Results may differ from a plain program's by a relative error of at most 0.0029.
Values may be sent and summed in bfloat16 or wider, within the bound.
No kernel may reach another device: no remote copies, remote signals or barrier semaphores. Data moves between devices by JAX's collectives and lax.ppermute only.
A program may use at most 64 MiB of HBM per device.

v0:
```python
import math
import jax
import jax.numpy as jnp
from jax import lax
from jax.sharding import PartitionSpec as P

STEP = 1000
beta_one = 0.9
beta_two = 0.999
epsilon = 1e-08


def on_device(inputs, out_grad, weight, proj_basis, first_moment, second_moment):
    tok_rows = inputs.shape[0]
    data_count = lax.axis_size("dp")
    shard_count = lax.axis_size("fsdp")
    rank_cols = proj_basis.shape[1]
    feature_grad = lax.dot_general(
        lax.all_gather(out_grad, "fsdp", axis=0, tiled=True),
        weight,
        (((1,), (1,)), ((), ())),
        preferred_element_type=jnp.float32,
    ).astype(jnp.bfloat16)
    input_grad = lax.all_to_all(feature_grad, "fsdp", split_axis=0, concat_axis=1, tiled=True)
    proj_full = jnp.dot(
        inputs,
        lax.all_gather(proj_basis, "fsdp", axis=0, tiled=True),
        preferred_element_type=jnp.float32,
    )
    projected_in = proj_full.astype(jnp.bfloat16)
    scale_factor = 1.0 / math.sqrt(tok_rows * data_count * shard_count)
    low_rank = (
        lax.dot_general(
            projected_in, out_grad, (((0,), (0,)), ((), ())), preferred_element_type=jnp.float32
        )
        * scale_factor
    )
    col_width = low_rank.shape[1] // data_count
    summed = lax.psum(low_rank, ("dp", "fsdp"))
    grad_block = lax.dynamic_slice_in_dim(summed, lax.axis_index("dp") * col_width, col_width, 1)
    flat_grad = grad_block.reshape(1, rank_cols * col_width)
    new_first = beta_one * first_moment + (1.0 - beta_one) * flat_grad
    new_second = beta_two * second_moment + (1.0 - beta_two) * flat_grad * flat_grad
    corr_one = 1.0 - beta_one**STEP
    corr_two = 1.0 - beta_two**STEP
    direction = (new_first / corr_one / (jnp.sqrt(new_second / corr_two) + epsilon)).astype(
        jnp.bfloat16
    )
    direction = direction.reshape(rank_cols, col_width)
    update = jnp.dot(proj_basis, direction, preferred_element_type=jnp.float32)
    return (input_grad, new_first, new_second, update)


def solution(mesh):
    in_specs = (
        P(("dp", "fsdp"), None),
        P(("dp", "fsdp"), None),
        P("fsdp", None),
        P("fsdp", None),
        P("dp", None),
        P("dp", None),
    )
    out_specs = (P(("dp", "fsdp"), None), P("dp", None), P("dp", None), P("fsdp", "dp"))
    return jax.shard_map(
        on_device, mesh=mesh, in_specs=in_specs, out_specs=out_specs, check_vma=False
    )
```

profile of v0, /device:TPU:1, one launch (start us, length us, event | category | flops | bytes accessed | tf_op | source)
XLA Modules:
  0.0 714.3 jit_solution(5845049301039747095)
XLA Ops:
  7.2 0.0 copy-start
  7.2 0.0 all-gather.3.cloned.1.call-start
  7.2 0.7 all-gather.3.cloned.1.call-update
  7.9 0.0 all-gather.5.cloned.1.call-start
  8.0 0.7 all-gather.5.cloned.1.call-update
  8.7 111.0 %all-gather.3.cloned.1.call-done = bf16[1024,2048]{1,0:T(8,128)(2,1)} async-done(((bf16[128,2048]{1,0:T(8,128)(2,1)}), bf16[1024,2048]{1,0:T(8,128)(2,1)}) %all-gather.3.cloned.1.call-update) | async-done | bytes 4194320 | tf_op jit(solution)/shard_map/all_gather | solution.py:19
  119.7 0.0 copy-done
  119.7 5.5 convolution_convert_fusion
  125.2 3.6 all-to-all-start
  128.8 0.0 all-reduce.2.cloned.1.call-start
  128.8 89.4 %all-gather.5.cloned.1.call-done = bf16[4096,256]{1,0:T(8,128)(2,1)} async-done(((bf16[512,256]{1,0:T(8,128)(2,1)}), bf16[4096,256]{1,0:T(8,128)(2,1)}) %all-gather.5.cloned.1.call-update) | async-done | bytes 2097168 | tf_op jit(solution)/shard_map/all_gather | solution.py:27
  218.2 4.7 convolution_multiply_fusion
  222.9 0.0 copy-start.1
  222.9 0.0 all-reduce.2.cloned.1.call-update
  222.9 478.2 %all-reduce.2.cloned.1.call-done = f32[256,2048]{0,1:T(8,128)} async-done(((f32[256,2048]{0,1:T(8,128)}), f32[256,2048]{0,1:T(8,128)}) %all-reduce.2.cloned.1.call-update) | async-done | bytes 2097168 | tf_op jit(solution)/shard_map/psum | solution.py:39
  701.2 1.4 constant_dynamic-slice_fusion
  702.5 0.9 copy.12
  703.4 0.7 reshape.53
  704.1 1.6 convert_reduce_fusion
  705.7 0.1 reshape.54
  705.8 0.0 copy-done.1
  705.8 0.8 convolution_bitcast_fusion
  706.7 0.0 all-to-all-done
  706.7 1.1 copy.13
Async XLA Ops:
  7.2 112.5 %copy-start = (bf16[512,2048]{1,0:T(8,128)(2,1)S(1)}, bf16[512,2048]{1,0:T(8,128)(2,1)}, u32[]{:S(2)}) copy-start(bf16[512,2048]{1,0:T(8,128)(2,1)} %param.8) | copy-start | bytes 6291460
  7.2 112.5 %all-gather.3.cloned.1.call-start = ((), (), s32[]{:S(2)}) async-start(), calls=%async_computation.1 | async-start | bytes 4718592 | tf_op jit(solution)/shard_map/all_gather | solution.py:19
  7.9 210.3 %all-gather.5.cloned.1.call-start = ((), (), s32[]{:S(2)}) async-start(), calls=%async_computation.2 | async-start | bytes 2359296 | tf_op jit(solution)/shard_map/all_gather | solution.py:27
  125.2 581.5 %all-to-all-start = ((bf16[8,128,512]{2,1,0:T(8,128)(2,1)}), bf16[8,128,512]{2,1,0:T(8,128)(2,1)S(1)}, u32[]{:S(2)}, u32[]{:S(2)}) async-start(bf16[8,128,512]{2,1,0:T(8,128)(2,1)} %bitcast.14), calls=%async_computation | async-start | bytes 2097152 | tf_op jit(solution)/shard_map/all_to_all | solution.py:24
  128.8 572.4 %all-reduce.2.cloned.1.call-start = ((), (), s32[]{:S(2)}) async-start(), calls=%async_computation.3 | async-start | bytes 4194304 | tf_op jit(solution)/shard_map/psum | solution.py:39
  222.9 482.9 %copy-start.1 = (bf16[512,256]{1,0:T(8,128)(2,1)S(1)}, bf16[512,256]{1,0:T(8,128)(2,1)}, u32[]{:S(2)}) copy-start(bf16[512,256]{1,0:T(8,128)(2,1)} %param.9) | copy-start | bytes 786436
Sparse Core Ops, SparseCore 0:
  10.1 109.5 all-gather.2
  121.8 96.4 all-gather.4
  223.6 477.5 all-reduce.1
where the time goes:
time: 715 us; the launch traced here: 714 us
  waiting for transfers between devices  680 us (95%)
  between operations  13.8 us (2%)
  matrix products  11 us (2%)
    psum x1, waiting for transfers between devices, on_device(): summed = lax.psum(low_rank, ('dp', 'fsdp'))  478 us
    all_gather x1, waiting for transfers between devices, on_device(): lax.all_gather(out_grad, 'fsdp', axis=0, tiled=True)  111 us
    all_gather x1, waiting for transfers between devices, on_device(): lax.all_gather(proj_basis, 'fsdp', axis=0, tiled=True)  89.4 us
  transfers between devices with their start and end apart: 4, of which 3 were waited for; matrix products, arithmetic and copies ran while one was open for 2% of the time, Pallas kernels for 0%

commit v1 on v0

--- a/solution.py
+++ b/solution.py
@@ -24,7 +24,9 @@
     input_grad = lax.all_to_all(feature_grad, "fsdp", split_axis=0, concat_axis=1, tiled=True)
     proj_full = jnp.dot(
         inputs,
-        lax.all_gather(proj_basis, "fsdp", axis=0, tiled=True),
+        jnp.concatenate(
+            lax.all_to_all(jnp.stack([proj_basis] * lax.axis_size("fsdp")), "fsdp", 0, 0), axis=0
+        ),
         preferred_element_type=jnp.float32,
     )
     projected_in = proj_full.astype(jnp.bfloat16)

time: 715 us -> 715 us (level)
  waiting for transfers between devices: 680 us -> 656 us
  starting transfers between devices: 3.68 us -> 24.4 us
    all_gather x1 -> x0, waiting for transfers between devices: 89.4 us -> none  [on_device(): lax.all_gather(proj_basis, 'fsdp', axis=0, tiled=True)]
    all_gather x1, waiting for transfers between devices: 111 us -> 168 us  [on_device(): lax.all_gather(out_grad, 'fsdp', axis=0, tiled=True)]
    all_to_all x0 -> x1, starting transfers between devices: none -> 13.1 us  [on_device(): lax.all_to_all(jnp.stack([proj_basis] * lax.axis_size('fsdp')), 'fsdp', 0...]
    psum x1, waiting for transfers between devices: 478 us -> 488 us  [on_device(): summed = lax.psum(low_rank, ('dp', 'fsdp'))]
    all_to_all x1, starting transfers between devices: 3.56 us -> 11.2 us  [on_device(): lax.all_to_all(feature_grad, 'fsdp', split_axis=0, concat_axis=1, tiled=T...]
  transfers between devices with their start and end apart: 4 -> 4, of which waited for: 3 -> 2; matrix products, arithmetic and copies ran while one was open for 2% -> 3% of each run, Pallas kernels for 0% -> 0%
where the time goes in v1:
time: 715 us
  waiting for transfers between devices  656 us (92%)
  starting transfers between devices  24.4 us (3%)
  between operations  15.5 us (2%)
  matrix products  11 us (2%)
    psum x1, waiting for transfers between devices, on_device(): summed = lax.psum(low_rank, ('dp', 'fsdp'))  488 us
    all_gather x1, waiting for transfers between devices, on_device(): lax.all_gather(out_grad, 'fsdp', axis=0, tiled=True)  168 us
  transfers between devices with their start and end apart: 4, of which 2 were waited for; matrix products, arithmetic and copies ran while one was open for 3% of the time, Pallas kernels for 0%

profile of v1, /device:TPU:1, one launch (start us, length us, event | category | flops | bytes accessed | tf_op | source)
XLA Modules:
  0.0 714.9 jit_solution(16595472634504363998)
XLA Ops:
  8.0 0.0 copy-start
  8.0 0.0 all-gather.2.cloned.1.call-start
  8.1 0.7 all-gather.2.cloned.1.call-update
  8.7 2.4 stack.2
  11.2 13.1 %all-to-all-start.1 = ((bf16[8,512,256]{2,1,0:T(8,128)(2,1)}), bf16[8,512,256]{2,1,0:T(8,128)(2,1)}, u32[]{:S(2)}, u32[]{:S(2)}) async-start(bf16[8,512,256]{2,1,0:T(8,128)(2,1)} %stack.2), calls=%async_computation.1 | async-start | bytes 4194304 | tf_op jit(solution)/shard_map/all_to_all | solution.py:28
  24.3 167.5 %all-gather.2.cloned.1.call-done = bf16[1024,2048]{1,0:T(8,128)(2,1)} async-done(((bf16[128,2048]{1,0:T(8,128)(2,1)}), bf16[1024,2048]{1,0:T(8,128)(2,1)}) %all-gather.2.cloned.1.call-update) | async-done | bytes 4194320 | tf_op jit(solution)/shard_map/all_gather | solution.py:19
  191.8 0.0 copy-done
  191.8 5.5 convolution_convert_fusion
  197.3 0.0 all-to-all-done.1
  197.3 11.2 %all-to-all-start = ((bf16[8,128,512]{2,1,0:T(8,128)(2,1)}), bf16[8,128,512]{2,1,0:T(8,128)(2,1)S(1)}, u32[]{:S(2)}, u32[]{:S(2)}) async-start(bf16[8,128,512]{2,1,0:T(8,128)(2,1)} %bitcast.15), calls=%async_computation | async-start | bytes 2097152 | tf_op jit(solution)/shard_map/all_to_all | solution.py:24
  208.5 0.0 all-reduce.2.cloned.1.call-start
  208.6 4.7 convolution_multiply_fusion
  213.3 0.0 copy-start.1
  213.3 0.0 all-reduce.2.cloned.1.call-update
  213.3 487.6 %all-reduce.2.cloned.1.call-done = f32[256,2048]{0,1:T(8,128)} async-done(((f32[256,2048]{0,1:T(8,128)}), f32[256,2048]{0,1:T(8,128)}) %all-reduce.2.cloned.1.call-update) | async-done | bytes 2097168 | tf_op jit(solution)/shard_map/psum | solution.py:41
  700.9 1.4 constant_dynamic-slice_fusion
  702.2 0.9 copy.12
  703.1 0.7 reshape.59
  703.8 1.6 convert_reduce_fusion
  705.4 0.1 reshape.60
  705.5 0.0 copy-done.1
  705.5 0.8 convolution_bitcast_fusion
  706.3 0.0 all-to-all-done
  706.4 1.1 copy.13
Async XLA Ops:
  8.0 183.8 %copy-start = (bf16[512,2048]{1,0:T(8,128)(2,1)S(1)}, bf16[512,2048]{1,0:T(8,128)(2,1)}, u32[]{:S(2)}) copy-start(bf16[512,2048]{1,0:T(8,128)(2,1)} %param.8) | copy-start | bytes 6291460
  8.0 183.8 %all-gather.2.cloned.1.call-start = ((), (), s32[]{:S(2)}) async-start(), calls=%async_computation.2 | async-start | bytes 4718592 | tf_op jit(solution)/shard_map/all_gather | solution.py:19
  11.2 186.1 %all-to-all-start.1 = ((bf16[8,512,256]{2,1,0:T(8,128)(2,1)}), bf16[8,512,256]{2,1,0:T(8,128)(2,1)}, u32[]{:S(2)}, u32[]{:S(2)}) async-start(bf16[8,512,256]{2,1,0:T(8,128)(2,1)} %stack.2), calls=%async_computation.1 | async-start | bytes 4194304 | tf_op jit(solution)/shard_map/all_to_all | solution.py:28
  197.3 509.0 %all-to-all-start = ((bf16[8,128,512]{2,1,0:T(8,128)(2,1)}), bf16[8,128,512]{2,1,0:T(8,128)(2,1)S(1)}, u32[]{:S(2)}, u32[]{:S(2)}) async-start(bf16[8,128,512]{2,1,0:T(8,128)(2,1)} %bitcast.15), calls=%async_computation | async-start | bytes 2097152 | tf_op jit(solution)/shard_map/all_to_all | solution.py:24
  208.5 492.3 %all-reduce.2.cloned.1.call-start = ((), (), s32[]{:S(2)}) async-start(), calls=%async_computation.3 | async-start | bytes 4194304 | tf_op jit(solution)/shard_map/psum | solution.py:41
  213.3 492.3 %copy-start.1 = (bf16[512,256]{1,0:T(8,128)(2,1)S(1)}, bf16[512,256]{1,0:T(8,128)(2,1)}, u32[]{:S(2)}) copy-start(bf16[512,256]{1,0:T(8,128)(2,1)} %param.9) | copy-start | bytes 786436
Sparse Core Ops, SparseCore 0:
  10.9 180.8 all-gather.1
Sparse Core Ops, SparseCore 1:
  214.4 486.4 all-reduce.1

commit v2 on v0

--- a/solution.py
+++ b/solution.py
@@ -36,7 +36,7 @@
         * scale_factor
     )
     col_width = low_rank.shape[1] // data_count
-    summed = lax.psum(low_rank, ("dp", "fsdp"))
+    summed = lax.psum(lax.psum(low_rank, "dp"), "fsdp")
     grad_block = lax.dynamic_slice_in_dim(summed, lax.axis_index("dp") * col_width, col_width, 1)
     flat_grad = grad_block.reshape(1, rank_cols * col_width)
     new_first = beta_one * first_moment + (1.0 - beta_one) * flat_grad

time: 715 us -> 1440 us (2.01)
  waiting for transfers between devices: 680 us -> 1410 us
    psum x1 -> x2, waiting for transfers between devices: 478 us -> 1230 us  [on_device(): summed = lax.psum(lax.psum(low_rank, 'dp'), 'fsdp')]
    all_gather x1, waiting for transfers between devices: 89.4 us -> 72.6 us  [on_device(): lax.all_gather(proj_basis, 'fsdp', axis=0, tiled=True)]
  transfers between devices with their start and end apart: 4 -> 5, of which waited for: 3 -> 4; matrix products, arithmetic and copies ran while one was open for 2% -> 1% of each run, Pallas kernels for 0% -> 0%
where the time goes in v2:
time: 1440 us
  waiting for transfers between devices  1410 us (98%)
    psum x2, waiting for transfers between devices, on_device(): summed = lax.psum(lax.psum(low_rank, 'dp'), 'fsdp')  1230 us
    all_gather x1, waiting for transfers between devices, on_device(): lax.all_gather(out_grad, 'fsdp', axis=0, tiled=True)  103 us
    all_gather x1, waiting for transfers between devices, on_device(): lax.all_gather(proj_basis, 'fsdp', axis=0, tiled=True)  72.6 us
  transfers between devices with their start and end apart: 5, of which 4 were waited for; matrix products, arithmetic and copies ran while one was open for 1% of the time, Pallas kernels for 0%

profile of v2, /device:TPU:1, one launch (start us, length us, event | category | flops | bytes accessed | tf_op | source)
XLA Modules:
  0.0 1440.2 jit_solution(15756059441815510310)
XLA Ops:
  7.2 0.0 copy-start
  7.2 0.0 all-gather.5.cloned.1.call-start
  7.2 0.7 all-gather.5.cloned.1.call-update
  7.9 0.0 all-gather.3.cloned.1.call-start
  8.0 0.7 all-gather.3.cloned.1.call-update
  8.7 0.0 all-reduce.3.cloned.1.call-start
  8.7 72.6 %all-gather.5.cloned.1.call-done = bf16[4096,256]{1,0:T(8,128)(2,1)} async-done(((bf16[512,256]{1,0:T(8,128)(2,1)}), bf16[4096,256]{1,0:T(8,128)(2,1)}) %all-gather.5.cloned.1.call-update) | async-done | bytes 2097168 | tf_op jit(solution)/shard_map/all_gather | solution.py:27
  81.3 4.7 convolution_multiply_fusion
  86.0 0.0 all-reduce.3.cloned.1.call-update
  86.0 102.5 %all-gather.3.cloned.1.call-done = bf16[1024,2048]{1,0:T(8,128)(2,1)} async-done(((bf16[128,2048]{1,0:T(8,128)(2,1)}), bf16[1024,2048]{1,0:T(8,128)(2,1)}) %all-gather.3.cloned.1.call-update) | async-done | bytes 4194320 | tf_op jit(solution)/shard_map/all_gather | solution.py:19
  188.5 5.5 convolution_convert_fusion
  194.0 3.7 all-to-all-start
  197.7 0.0 all-reduce.5.cloned.1.call-start
  197.8 1090.3 %all-reduce.3.cloned.1.call-done = f32[256,2048]{0,1:T(8,128)} async-done(((f32[256,2048]{0,1:T(8,128)}), f32[256,2048]{0,1:T(8,128)}) %all-reduce.3.cloned.1.call-update) | async-done | bytes 2097168 | tf_op jit(solution)/shard_map/psum | solution.py:39
  1288.1 0.0 all-reduce.5.cloned.1.call-update
  1288.1 139.0 %all-reduce.5.cloned.1.call-done = f32[256,2048]{0,1:T(8,128)} async-done(((f32[256,2048]{0,1:T(8,128)}), f32[256,2048]{0,1:T(8,128)}) %all-reduce.5.cloned.1.call-update) | async-done | bytes 2097168 | tf_op jit(solution)/shard_map/psum | solution.py:39
  1427.1 1.4 constant_dynamic-slice_fusion
  1428.5 0.9 copy.12
  1429.3 0.7 reshape.53
  1430.0 1.6 convert_reduce_fusion
  1431.7 0.1 reshape.54
  1431.8 0.8 convolution_bitcast_fusion
  1432.6 0.0 all-to-all-done
  1432.6 1.1 copy.13
  (3 shorter events, 0.0 us)
Async XLA Ops:
  7.2 181.3 %copy-start = (bf16[512,2048]{1,0:T(8,128)(2,1)S(1)}, bf16[512,2048]{1,0:T(8,128)(2,1)}, u32[]{:S(2)}) copy-start(bf16[512,2048]{1,0:T(8,128)(2,1)} %param.8) | copy-start | bytes 6291460
  7.2 74.1 %all-gather.5.cloned.1.call-start = ((), (), s32[]{:S(2)}) async-start(), calls=%async_computation.2 | async-start | bytes 2359296 | tf_op jit(solution)/shard_map/all_gather | solution.py:27
  7.9 180.6 %all-gather.3.cloned.1.call-start = ((), (), s32[]{:S(2)}) async-start(), calls=%async_computation.1 | async-start | bytes 4718592 | tf_op jit(solution)/shard_map/all_gather | solution.py:19
  8.7 1279.4 %all-reduce.3.cloned.1.call-start = ((), (), s32[]{:S(2)}) async-start(), calls=%async_computation.3 | async-start | bytes 4194304 | tf_op jit(solution)/shard_map/psum | solution.py:39
  194.0 1237.7 %copy-start.1 = (bf16[512,256]{1,0:T(8,128)(2,1)S(1)}, bf16[512,256]{1,0:T(8,128)(2,1)}, u32[]{:S(2)}) copy-start(bf16[512,256]{1,0:T(8,128)(2,1)} %param.9) | copy-start | bytes 786436
  194.0 1238.6 %all-to-all-start = ((bf16[8,128,512]{2,1,0:T(8,128)(2,1)}), bf16[8,128,512]{2,1,0:T(8,128)(2,1)S(1)}, u32[]{:S(2)}, u32[]{:S(2)}) async-start(bf16[8,128,512]{2,1,0:T(8,128)(2,1)} %bitcast.14), calls=%async_computation | async-start | bytes 2097152 | tf_op jit(solution)/shard_map/all_to_all | solution.py:24
  197.7 1229.4 %all-reduce.5.cloned.1.call-start = ((), (), s32[]{:S(2)}) async-start(), calls=%async_computation.4 | async-start | bytes 4194304 | tf_op jit(solution)/shard_map/psum | solution.py:39
Sparse Core Ops, SparseCore 0:
  10.1 71.1 all-gather.4
  83.3 105.0 all-gather.2
  191.4 1096.6 all-reduce.2
  1291.1 135.8 all-reduce.4
